TPU v7x, 32 devices: a whole 2x2x4 slice. The times are simulated.
32 devices in a mesh: rep: 2 (over core), shard: 16 (over z, y, x).
Axes of the slice: x: 2, y: 2, z: 4, core: 2. Of those that a mesh axis runs over, the one named last changes fastest.
Arguments:
- tokens: bfloat16 [12288, 1536], P(('rep', 'shard')), may hold values from -6 to 6
- prompt_ids: int32 [32, 4], P(('rep', 'shard')), may hold values from 0 to 1
- seq_offsets: int32 [32, 4], P(('rep', 'shard')), may hold values from 32 to 64, as said below
- attn_gain: bfloat16 [1536], P('shard'), may hold values from 0.5 to 1.5
- w_query: bfloat16 [1536, 1536], P('shard'), may hold values from -0.15625 to 0.15625
- w_key: bfloat16 [1536, 1536], P('shard'), may hold values from -0.15625 to 0.15625
- w_value: bfloat16 [1536, 1536], P('shard'), may hold values from -0.15625 to 0.15625
- w_outgate: bfloat16 [1536, 1536], P('shard'), may hold values from -0.15625 to 0.15625
- w_forget: bfloat16 [1536, 24], P('shard'), may hold values from -0.15625 to 0.15625
- forget_bias: bfloat16 [24], replicated, may hold values from 1 to 8
- w_output: bfloat16 [1536, 1536], P('shard'), may hold values from -0.625 to 0.625
- ffn_gain: bfloat16 [1536], P('shard'), may hold values from 0.5 to 1.5
- w_gate: bfloat16 [1536, 4096], P('shard'), may hold values from -0.15625 to 0.15625
- w_up: bfloat16 [1536, 4096], P('shard'), may hold values from -0.15625 to 0.15625
- w_down: bfloat16 [4096, 1536], P('shard'), may hold values from -0.09375 to 0.09375
- cotangent: bfloat16 [12288, 1536], P(('rep', 'shard')), may hold values from -6 to 6
Outputs:
- layer_out: bfloat16 [12288, 1536], P(('rep', 'shard'))
- tokens_grad: float32 [12288, 1536], P(('rep', 'shard'))
- attn_gain_grad: float32 [1536], P('shard')
- query_grad: float32 [1536, 1536], P('shard')
- key_grad: float32 [1536, 1536], P('shard')
- value_grad: float32 [1536, 1536], P('shard')
- outgate_grad: float32 [1536, 1536], P('shard')
- forget_grad: float32 [1536, 24], P('shard')
- forget_bias_grad: float32 [24], replicated
- output_grad: float32 [1536, 1536], P('shard')
- ffn_gain_grad: float32 [1536], P('shard')
- gate_grad: float32 [1536, 4096], P('shard')
- up_grad: float32 [1536, 4096], P('shard')
- down_grad: float32 [4096, 1536], P('shard')
Inputs may be any that keep to these rules, and one draw needn't show every extreme that they name: `prompt_ids`: each continuation follows one of the 2 prompts of its own block. `seq_offsets`: in every block at least one continuation follows its whole prompt.
All inputs are finite; a program needn't handle non-finite values.
Results may differ from a plain program's by a relative error of at most 0.023.
Values may be sent and summed in bfloat16 or wider, within the bound.
No kernel may reach another device: no remote copies, remote signals or barrier semaphores. Data moves between devices by JAX's collectives and lax.ppermute only.
A program may use at most 320 MiB of HBM per device.

v0:
```python
import jax
import jax.numpy as jnp
from jax import lax
from jax.sharding import PartitionSpec as P

PLEN = 64
CLEN = 64
NP = 2
NC = 4
EPS = 1e-06
NEGATIVE = -1e30


def chain_mask(prompt_ids, offsets):
    positions = jnp.arange(NP * PLEN + NC * CLEN, dtype=jnp.int32)
    in_prompt = positions < NP * PLEN
    after_prompts = positions - NP * PLEN
    sequence = jnp.where(in_prompt, positions // PLEN, NP + after_prompts // CLEN)
    within = jnp.where(in_prompt, positions % PLEN, after_prompts % CLEN)
    cont_index = sequence - NP
    selector = (cont_index[:, None] == jnp.arange(NC, dtype=jnp.int32)[None, :]).astype(jnp.int32)
    owner_id = jnp.where(in_prompt, -1, jnp.sum(selector * prompt_ids[None, :], axis=1))
    reach_end = jnp.sum(selector * offsets[None, :], axis=1)
    same_seq = (sequence[:, None] == sequence[None, :]) & (within[None, :] <= within[:, None])
    from_prompt = (owner_id[:, None] == sequence[None, :]) & (within[None, :] < reach_end[:, None])
    return same_seq | from_prompt


def normalize(values):
    inverse = lax.rsqrt(jnp.mean(values * values, axis=1, keepdims=True) + EPS)
    return (values * inverse, inverse)


def norm_back(grad_scaled, scaled, inverse):
    return inverse * (grad_scaled - scaled * jnp.mean(grad_scaled * scaled, axis=1, keepdims=True))


def matmul(left_side, right_side):
    return jnp.dot(left_side, right_side, preferred_element_type=jnp.float32)


def matmul_tn(left_side, right_side):
    return lax.dot_general(
        left_side, right_side, (((0,), (0,)), ((), ())), preferred_element_type=jnp.float32
    )


def matmul_nt(left_side, right_side):
    return lax.dot_general(
        left_side, right_side, (((1,), (1,)), ((), ())), preferred_element_type=jnp.float32
    )


def decayed_scores(query_low, key_low, decay_sum, chain_ok, score_scale):
    logits = jnp.einsum("qhd,khd->hqk", query_low, key_low, preferred_element_type=jnp.float32)
    decay_t = decay_sum.T
    logits = logits * score_scale + decay_t[:, :, None] - decay_t[:, None, :]
    return jnp.where(chain_ok[None, :, :], logits, NEGATIVE)


def local(
    tokens,
    prompt_ids,
    seq_offsets,
    attn_gain,
    w_query,
    w_key,
    w_value,
    w_outgate,
    w_forget,
    forget_bias,
    w_output,
    ffn_gain,
    w_gate,
    w_up,
    w_down,
    cotangent,
):
    row_count = tokens.shape[0]
    model_width = tokens.shape[1]
    head_count = w_forget.shape[1]
    head_dim = model_width // head_count
    score_scale = head_dim ** (-0.5)
    chain_ok = chain_mask(prompt_ids[0], seq_offsets[0])
    chain_float = chain_ok.astype(jnp.float32)
    inputs = tokens.astype(jnp.float32)
    scaled1, inverse1 = normalize(inputs)
    gain_part = lax.all_gather(attn_gain, "shard", axis=0, tiled=True)
    query_part = lax.all_gather(w_query, "shard", axis=0, tiled=True)
    key_part = lax.all_gather(w_key, "shard", axis=0, tiled=True)
    value_part = lax.all_gather(w_value, "shard", axis=0, tiled=True)
    outgate_part = lax.all_gather(w_outgate, "shard", axis=0, tiled=True)
    forget_part = lax.all_gather(w_forget, "shard", axis=0, tiled=True)
    normed_part = (scaled1 * gain_part.astype(jnp.float32)).astype(jnp.bfloat16)
    gain_one = gain_part
    normed1 = normed_part
    query_proj = matmul(normed_part, query_part)
    key_proj = matmul(normed_part, key_part)
    value_proj = matmul(normed_part, value_part)
    outgate_pre = matmul(normed_part, outgate_part)
    forget_pre = matmul(normed_part, forget_part)
    query_low = query_proj.astype(jnp.bfloat16).reshape(row_count, head_count, head_dim)
    key_low = key_proj.astype(jnp.bfloat16).reshape(row_count, head_count, head_dim)
    value_low = value_proj.astype(jnp.bfloat16).reshape(row_count, head_count, head_dim)
    forget_in = forget_pre + forget_bias.astype(jnp.float32)[None, :]
    decay_sum = jnp.dot(chain_float, jax.nn.log_sigmoid(forget_in), precision=lax.Precision.HIGHEST)
    logits = decayed_scores(query_low, key_low, decay_sum, chain_ok, score_scale)
    top_score = jnp.max(logits, axis=2, keepdims=True)
    exp_scores = jnp.exp(logits - top_score)
    denominator = jnp.sum(exp_scores, axis=2, keepdims=True)
    log_total = top_score + jnp.log(denominator)
    probs_low = (exp_scores / denominator).astype(jnp.bfloat16)
    attended = jnp.einsum(
        "hqk,khd->qhd", probs_low, value_low, preferred_element_type=jnp.float32
    ).reshape(row_count, model_width)
    gate_open = jax.nn.sigmoid(outgate_pre)
    gated_low = (attended * gate_open).astype(jnp.bfloat16)
    branch_attn = matmul(gated_low, lax.all_gather(w_output, "shard", axis=0, tiled=True))
    residual = inputs + branch_attn
    scaled2, inverse2 = normalize(residual)
    gain_part = lax.all_gather(ffn_gain, "shard", axis=0, tiled=True)
    gate_part = lax.all_gather(w_gate, "shard", axis=0, tiled=True)
    up_part = lax.all_gather(w_up, "shard", axis=0, tiled=True)
    normed_part = (scaled2 * gain_part.astype(jnp.float32)).astype(jnp.bfloat16)
    gate_pre = matmul(normed_part, gate_part)
    up_pre = matmul(normed_part, up_part)
    sig_gate = jax.nn.sigmoid(gate_pre)
    silu_gate = gate_pre * sig_gate
    act_low = (silu_gate * up_pre).astype(jnp.bfloat16)
    branch_ffn = matmul(act_low, lax.all_gather(w_down, "shard", axis=0, tiled=True))
    layer_out = (residual + branch_ffn).astype(jnp.bfloat16)
    grad_out = cotangent.astype(jnp.float32)
    grad_act = matmul_nt(cotangent, lax.all_gather(w_down, "shard", axis=0, tiled=True))
    grad_gate = (grad_act * up_pre * sig_gate * (1.0 + gate_pre * (1.0 - sig_gate))).astype(
        jnp.bfloat16
    )
    grad_up = (grad_act * silu_gate).astype(jnp.bfloat16)
    gate_part = lax.all_gather(w_gate, "shard", axis=0, tiled=True)
    up_part = lax.all_gather(w_up, "shard", axis=0, tiled=True)
    contribution = matmul_nt(grad_gate, gate_part) + matmul_nt(grad_up, up_part)
    grad_normed2 = contribution
    grad_down = matmul_tn(act_low, cotangent)
    grad_gate_w = matmul_tn(normed_part, grad_gate)
    grad_up_w = matmul_tn(normed_part, grad_up)
    grad_gain2 = jnp.sum(grad_normed2 * scaled2, axis=0)
    ffn_parts = (
        lax.psum_scatter(
            grad_gain2.astype(jnp.bfloat16), "shard", scatter_dimension=0, tiled=True
        ).astype(jnp.float32),
        lax.psum_scatter(
            grad_gate_w.astype(jnp.bfloat16), "shard", scatter_dimension=0, tiled=True
        ).astype(jnp.float32),
        lax.psum_scatter(
            grad_up_w.astype(jnp.bfloat16), "shard", scatter_dimension=0, tiled=True
        ).astype(jnp.float32),
        lax.psum_scatter(
            grad_down.astype(jnp.bfloat16), "shard", scatter_dimension=0, tiled=True
        ).astype(jnp.float32),
    )
    grad_resid = grad_out + norm_back(
        grad_normed2 * gain_part.astype(jnp.float32), scaled2, inverse2
    )
    grad_attn = grad_resid.astype(jnp.bfloat16)
    grad_gated = matmul_nt(grad_attn, lax.all_gather(w_output, "shard", axis=0, tiled=True))
    grad_output_w = matmul_tn(gated_low, grad_attn)
    grad_attended = (
        (grad_gated * gate_open).astype(jnp.bfloat16).reshape(row_count, head_count, head_dim)
    )
    grad_outgate = (grad_gated * attended * gate_open * (1.0 - gate_open)).astype(jnp.bfloat16)
    logits = decayed_scores(query_low, key_low, decay_sum, chain_ok, score_scale)
    prob_full = jnp.exp(logits - log_total)
    prob_again = prob_full.astype(jnp.bfloat16)
    grad_probs = jnp.einsum(
        "qhd,khd->hqk", grad_attended, value_low, preferred_element_type=jnp.float32
    )
    grad_value = jnp.einsum(
        "hqk,qhd->khd", prob_again, grad_attended, preferred_element_type=jnp.float32
    )
    grad_logits = prob_full * (grad_probs - jnp.sum(prob_full * grad_probs, axis=2, keepdims=True))
    grad_qk = (grad_logits * score_scale).astype(jnp.bfloat16)
    grad_query = jnp.einsum("hqk,khd->qhd", grad_qk, key_low, preferred_element_type=jnp.float32)
    grad_key = jnp.einsum("hqk,qhd->khd", grad_qk, query_low, preferred_element_type=jnp.float32)
    grad_decay = (jnp.sum(grad_logits, axis=2) - jnp.sum(grad_logits, axis=1)).T
    grad_log_forget = lax.dot_general(
        chain_float, grad_decay, (((0,), (0,)), ((), ())), precision=lax.Precision.HIGHEST
    )
    grad_forget_in = grad_log_forget * jax.nn.sigmoid(-forget_in)
    grad_bias = lax.psum(jnp.sum(grad_forget_in, axis=0), ("rep", "shard"))
    grad_query_low = grad_query.reshape(row_count, model_width).astype(jnp.bfloat16)
    grad_key_low = grad_key.reshape(row_count, model_width).astype(jnp.bfloat16)
    grad_value_low = grad_value.reshape(row_count, model_width).astype(jnp.bfloat16)
    grad_forget_low = grad_forget_in.astype(jnp.bfloat16)
    query_part = lax.all_gather(w_query, "shard", axis=0, tiled=True)
    key_part = lax.all_gather(w_key, "shard", axis=0, tiled=True)
    value_part = lax.all_gather(w_value, "shard", axis=0, tiled=True)
    outgate_part = lax.all_gather(w_outgate, "shard", axis=0, tiled=True)
    forget_part = lax.all_gather(w_forget, "shard", axis=0, tiled=True)
    contribution = (
        matmul_nt(grad_query_low, query_part)
        + matmul_nt(grad_key_low, key_part)
        + matmul_nt(grad_value_low, value_part)
        + matmul_nt(grad_outgate, outgate_part)
        + matmul_nt(grad_forget_low, forget_part)
    )
    grad_query_w = matmul_tn(normed1, grad_query_low)
    grad_key_w = matmul_tn(normed1, grad_key_low)
    grad_value_w = matmul_tn(normed1, grad_value_low)
    grad_outgate_w = matmul_tn(normed1, grad_outgate)
    grad_forget_w = matmul_tn(normed1, grad_forget_low)
    grad_gain1 = jnp.sum(contribution * scaled1, axis=0)
    grad_inputs = grad_resid + norm_back(
        contribution * gain_one.astype(jnp.float32), scaled1, inverse1
    )
    attn_parts = (
        lax.psum_scatter(
            grad_gain1.astype(jnp.bfloat16), "shard", scatter_dimension=0, tiled=True
        ).astype(jnp.float32),
        lax.psum_scatter(
            grad_query_w.astype(jnp.bfloat16), "shard", scatter_dimension=0, tiled=True
        ).astype(jnp.float32),
        lax.psum_scatter(
            grad_key_w.astype(jnp.bfloat16), "shard", scatter_dimension=0, tiled=True
        ).astype(jnp.float32),
        lax.psum_scatter(
            grad_value_w.astype(jnp.bfloat16), "shard", scatter_dimension=0, tiled=True
        ).astype(jnp.float32),
        lax.psum_scatter(
            grad_outgate_w.astype(jnp.bfloat16), "shard", scatter_dimension=0, tiled=True
        ).astype(jnp.float32),
        lax.psum_scatter(
            grad_forget_w.astype(jnp.bfloat16), "shard", scatter_dimension=0, tiled=True
        ).astype(jnp.float32),
        lax.psum_scatter(
            grad_output_w.astype(jnp.bfloat16), "shard", scatter_dimension=0, tiled=True
        ).astype(jnp.float32),
    )
    summed = (
        lax.psum(attn_parts[0].astype(jnp.bfloat16), "rep").astype(jnp.float32),
        lax.psum(attn_parts[1].astype(jnp.bfloat16), "rep").astype(jnp.float32),
        lax.psum(attn_parts[2].astype(jnp.bfloat16), "rep").astype(jnp.float32),
        lax.psum(attn_parts[3].astype(jnp.bfloat16), "rep").astype(jnp.float32),
        lax.psum(attn_parts[4].astype(jnp.bfloat16), "rep").astype(jnp.float32),
        lax.psum(attn_parts[5].astype(jnp.bfloat16), "rep").astype(jnp.float32),
        lax.psum(attn_parts[6].astype(jnp.bfloat16), "rep").astype(jnp.float32),
        lax.psum(ffn_parts[0].astype(jnp.bfloat16), "rep").astype(jnp.float32),
        lax.psum(ffn_parts[1].astype(jnp.bfloat16), "rep").astype(jnp.float32),
        lax.psum(ffn_parts[2].astype(jnp.bfloat16), "rep").astype(jnp.float32),
        lax.psum(ffn_parts[3].astype(jnp.bfloat16), "rep").astype(jnp.float32),
    )
    return (
        layer_out,
        grad_inputs,
        summed[0],
        summed[1],
        summed[2],
        summed[3],
        summed[4],
        summed[5],
        grad_bias,
        summed[6],
        summed[7],
        summed[8],
        summed[9],
        summed[10],
    )


def solution(mesh):
    in_specs = (
        P(("rep", "shard"), None),
        P(("rep", "shard"), None),
        P(("rep", "shard"), None),
        P("shard"),
        P("shard", None),
        P("shard", None),
        P("shard", None),
        P("shard", None),
        P("shard", None),
        P(),
        P("shard", None),
        P("shard"),
        P("shard", None),
        P("shard", None),
        P("shard", None),
        P(("rep", "shard"), None),
    )
    out_specs = (
        P(("rep", "shard"), None),
        P(("rep", "shard"), None),
        P("shard"),
        P("shard", None),
        P("shard", None),
        P("shard", None),
        P("shard", None),
        P("shard", None),
        P(),
        P("shard", None),
        P("shard"),
        P("shard", None),
        P("shard", None),
        P("shard", None),
    )
    return jax.shard_map(local, mesh=mesh, in_specs=in_specs, out_specs=out_specs, check_vma=False)
```

profile of v0, /device:TPU:0, one launch (start us, length us, event | category | flops | bytes accessed | tf_op | source)
XLA Modules:
  0.0 2422.7 jit_solution(16868182657455146212)
XLA Ops:
  14.6 45.2 %all-reduce.5 = (bf16[1536]{0:T(1024)(128)(2,1)S(1)}, bf16[1536]{0:T(1024)(128)(2,1)S(1)}) all-reduce(bf16[1536]{0:T(1024)(128)(2,1)S(1)} %dynamic-update-slice, bf16[1536]{0:T(1024)(128)(2,1)S(1)} %dynamic-update-slice.1), channel_id=1, replica_groups=mesh['rep'=2,'shard'=16] {'shard'}, use_global_device_ids=true, to_apply=%add | all-reduce | flops 3072 | bytes 12288
  59.8 37.5 %all-gather = bf16[16,96,24]{1,2,0:T(8,128)(2,1)S(1)} all-gather(bf16[1,96,24]{1,2,0:T(8,128)(2,1)S(1)} %bitcast.93), channel_id=1, replica_groups=mesh['rep'=2,'shard'=16] {'shard'}, dimensions={0}, use_global_device_ids=true | all-gather | bytes 78336 | tf_op jit(solution)/shard_map/all_gather | solution.py:93
  105.3 71.1 %all-gather.14.cloned.1.call-done = bf16[1536,1536]{1,0:T(8,128)(2,1)} async-done(((bf16[96,1536]{1,0:T(8,128)(2,1)}), bf16[1536,1536]{1,0:T(8,128)(2,1)}) %all-gather.14.cloned.1.call-update) | async-done | bytes 4718608 | tf_op jit(solution)/shard_map/all_gather | solution.py:90
  183.5 74.1 %all-gather.10.cloned.1.call-done = bf16[1536,1536]{1,0:T(8,128)(2,1)} async-done(((bf16[96,1536]{1,0:T(8,128)(2,1)}), bf16[1536,1536]{1,0:T(8,128)(2,1)}) %all-gather.10.cloned.1.call-update) | async-done | bytes 4718608 | tf_op jit(solution)/shard_map/all_gather | solution.py:91
  292.0 46.6 %all-gather.16.cloned.1.call-done = bf16[1536,1536]{1,0:T(8,128)(2,1)} async-done(((bf16[96,1536]{1,0:T(8,128)(2,1)}), bf16[1536,1536]{1,0:T(8,128)(2,1)}) %all-gather.16.cloned.1.call-update) | async-done | bytes 4718608 | tf_op jit(solution)/shard_map/all_gather | solution.py:92
  345.1 74.6 %all-gather.18.cloned.1.call-done = bf16[1536,1536]{1,0:T(8,128)(2,1)} async-done(((bf16[96,1536]{1,0:T(8,128)(2,1)}), bf16[1536,1536]{1,0:T(8,128)(2,1)}) %all-gather.18.cloned.1.call-update) | async-done | bytes 4718608 | tf_op jit(solution)/shard_map/all_gather | solution.py:118
  426.4 146.0 %all-gather.22.cloned.1.call-done = bf16[1536,4096]{1,0:T(8,128)(2,1)} async-done(((bf16[96,4096]{1,0:T(8,128)(2,1)}), bf16[1536,4096]{1,0:T(8,128)(2,1)}) %all-gather.22.cloned.1.call-update) | async-done | bytes 12582928 | tf_op jit(solution)/shard_map/all_gather | solution.py:123
  582.3 142.5 %all-gather.20.cloned.1.call-done = bf16[1536,4096]{1,0:T(8,128)(2,1)} async-done(((bf16[96,4096]{1,0:T(8,128)(2,1)}), bf16[1536,4096]{1,0:T(8,128)(2,1)}) %all-gather.20.cloned.1.call-update) | async-done | bytes 12582928 | tf_op jit(solution)/shard_map/all_gather | solution.py:122
  734.7 142.5 %all-gather.24.cloned.1.call-done = bf16[4096,1536]{1,0:T(8,128)(2,1)} async-done(((bf16[256,1536]{1,0:T(8,128)(2,1)}), bf16[4096,1536]{1,0:T(8,128)(2,1)}) %all-gather.24.cloned.1.call-update) | async-done | bytes 12582928 | tf_op jit(solution)/shard_map/all_gather | solution.py:130
  877.2 15.0 multiply_convert_fusion.1
  948.4 22.3 fusion.83
  1008.5 11.3 convolution_convert_fusion.1
  1020.0 11.4 convolution_convert_fusion.2
  1048.1 38.9 %psum.90 = f32[24]{0:T(128)} all-reduce(f32[24]{0:T(128)S(1)} %get-tuple-element.53), channel_id=1, replica_groups=mesh['rep'=2,'shard'=16] {'rep','shard'}, use_global_device_ids=true, to_apply=%region_25.26 | all-reduce | flops 24 | bytes 192 | tf_op jit(solution)/shard_map/psum | solution.py:188
  1086.9 110.5 %reduce-scatter.18.cloned.1.call-done = bf16[96,1536]{1,0:T(8,128)(2,1)} async-done(((bf16[1536,1536]{1,0:T(8,128)(2,1)}), bf16[96,1536]{1,0:T(8,128)(2,1)}) %reduce-scatter.18.cloned.1.call-update) | async-done | bytes 294928 | tf_op jit(solution)/shard_map/reduce_scatter | solution.py:227
  1197.4 143.3 %reduce-scatter.16.cloned.1.call-done = bf16[96,1536]{1,0:T(8,128)(2,1)} async-done(((bf16[1536,1536]{1,0:T(8,128)(2,1)}), bf16[96,1536]{1,0:T(8,128)(2,1)}) %reduce-scatter.16.cloned.1.call-update) | async-done | bytes 294928 | tf_op jit(solution)/shard_map/reduce_scatter | solution.py:224
  1340.7 142.9 %reduce-scatter.14.cloned.1.call-done = bf16[96,1536]{1,0:T(8,128)(2,1)} async-done(((bf16[1536,1536]{1,0:T(8,128)(2,1)}), bf16[96,1536]{1,0:T(8,128)(2,1)}) %reduce-scatter.14.cloned.1.call-update) | async-done | bytes 294928 | tf_op jit(solution)/shard_map/reduce_scatter | solution.py:221
  1483.7 143.1 %reduce-scatter.12.cloned.1.call-done = bf16[96,1536]{1,0:T(8,128)(2,1)} async-done(((bf16[1536,1536]{1,0:T(8,128)(2,1)}), bf16[96,1536]{1,0:T(8,128)(2,1)}) %reduce-scatter.12.cloned.1.call-update) | async-done | bytes 294928 | tf_op jit(solution)/shard_map/reduce_scatter | solution.py:218
  1626.7 207.2 %reduce-scatter.26.cloned.1.call-done = bf16[256,1536]{1,0:T(8,128)(2,1)} async-done(((bf16[4096,1536]{1,0:T(8,128)(2,1)}), bf16[256,1536]{1,0:T(8,128)(2,1)}) %reduce-scatter.26.cloned.1.call-update) | async-done | bytes 786448 | tf_op jit(solution)/shard_map/reduce_scatter | solution.py:156
  1834.0 207.7 %reduce-scatter.24.cloned.1.call-done = bf16[96,4096]{1,0:T(8,128)(2,1)} async-done(((bf16[1536,4096]{1,0:T(8,128)(2,1)}), bf16[96,4096]{1,0:T(8,128)(2,1)}) %reduce-scatter.24.cloned.1.call-update) | async-done | bytes 786448 | tf_op jit(solution)/shard_map/reduce_scatter | solution.py:153
  2041.7 207.7 %reduce-scatter.22.cloned.1.call-done = bf16[96,4096]{1,0:T(8,128)(2,1)} async-done(((bf16[1536,4096]{1,0:T(8,128)(2,1)}), bf16[96,4096]{1,0:T(8,128)(2,1)}) %reduce-scatter.22.cloned.1.call-update) | async-done | bytes 786448 | tf_op jit(solution)/shard_map/reduce_scatter | solution.py:150
  2262.4 41.8 %all-reduce.4 = (bf16[1536]{0:T(1024)(128)(2,1)}, bf16[1536]{0:T(1024)(128)(2,1)}) all-reduce(bf16[1536]{0:T(1024)(128)(2,1)S(1)} %get-tuple-element.18, bf16[1536]{0:T(1024)(128)(2,1)} %get-tuple-element.16), channel_id=2, replica_groups=mesh['rep'=2,'shard'=16] {'shard'}, use_global_device_ids=true, to_apply=%region_12.13.clone | all-reduce | flops 3072 | bytes 12288
  2320.1 56.9 %reduce-scatter.28.cloned.1.call-done = bf16[96,24]{1,0:T(8,128)(2,1)} async-done(((bf16[1536,24]{1,0:T(8,128)(2,1)}), bf16[96,24]{1,0:T(8,128)(2,1)}) %reduce-scatter.28.cloned.1.call-update) | async-done | bytes 4624
  2382.0 22.1 all-reduce.10.cloned.1.call-done
  (199 shorter events, 243.7 us)
Async XLA Ops:
  7.2 90.3 %copy-start.33 = (s32[1,4]{1,0:T(1,128)S(1)}, s32[1,4]{1,0:T(1,128)}, u32[]{:S(2)}) copy-start(s32[1,4]{1,0:T(1,128)} %param.18) | copy-start | bytes 52
  7.2 90.3 %copy-start.32 = (s32[1,4]{1,0:T(1,128)S(1)}, s32[1,4]{1,0:T(1,128)}, u32[]{:S(2)}) copy-start(s32[1,4]{1,0:T(1,128)} %param.17) | copy-start | bytes 52
  7.3 90.4 %copy-start = (bf16[384,1536]{1,0:T(8,128)(2,1)S(1)}, bf16[384,1536]{1,0:T(8,128)(2,1)}, u32[]{:S(2)}) copy-start(bf16[384,1536]{1,0:T(8,128)(2,1)} %param.16) | copy-start | bytes 3538948
  7.3 92.6 %all-gather.12.cloned.1.call-start = ((), (), s32[]{:S(2)}) async-start(), calls=%async_computation.10 | async-start | bytes 5013504 | tf_op jit(solution)/shard_map/all_gather | solution.py:89
  8.0 168.4 %all-gather.14.cloned.1.call-start = ((), (), s32[]{:S(2)}) async-start(), calls=%async_computation.11 | async-start | bytes 5013504 | tf_op jit(solution)/shard_map/all_gather | solution.py:90
  8.7 248.8 %all-gather.10.cloned.1.call-start = ((), (), s32[]{:S(2)}) async-start(), calls=%async_computation.9 | async-start | bytes 5013504 | tf_op jit(solution)/shard_map/all_gather | solution.py:91
  9.5 329.1 %all-gather.16.cloned.1.call-start = ((), (), s32[]{:S(2)}) async-start(), calls=%async_computation.12 | async-start | bytes 5013504 | tf_op jit(solution)/shard_map/all_gather | solution.py:92
  10.1 409.6 %all-gather.18.cloned.1.call-start = ((), (), s32[]{:S(2)}) async-start(), calls=%async_computation.13 | async-start | bytes 5013504 | tf_op jit(solution)/shard_map/all_gather | solution.py:118
  10.6 561.7 %all-gather.22.cloned.1.call-start = ((), (), s32[]{:S(2)}) async-start(), calls=%async_computation.15 | async-start | bytes 13369344 | tf_op jit(solution)/shard_map/all_gather | solution.py:123
  11.2 713.6 %all-gather.20.cloned.1.call-start = ((), (), s32[]{:S(2)}) async-start(), calls=%async_computation.14 | async-start | bytes 13369344 | tf_op jit(solution)/shard_map/all_gather | solution.py:122
  12.0 865.2 %all-gather.24.cloned.1.call-start = ((), (), s32[]{:S(2)}) async-start(), calls=%async_computation.16 | async-start | bytes 13369344 | tf_op jit(solution)/shard_map/all_gather | solution.py:130
  12.7 1074.2 %reduce-scatter.20.cloned.1.call-start = ((), (), s32[]{:S(2)}) async-start(), calls=%async_computation.21 | async-start | bytes 5013504 | tf_op jit(solution)/shard_map/reduce_scatter | solution.py:233
  105.2 160.1 %copy-start.5 = (bf16[384,1536]{0,1:T(8,128)(2,1)}, bf16[384,1536]{0,1:T(8,128)(2,1)S(1)}, u32[]{:S(2)}) copy-start(bf16[384,1536]{0,1:T(8,128)(2,1)S(1)} %copy.67) | copy-start | bytes 3538948
  183.5 81.9 %copy-start.4 = (bf16[384,1536]{0,1:T(8,128)(2,1)}, bf16[384,1536]{0,1:T(8,128)(2,1)S(1)}, u32[]{:S(2)}) copy-start(bf16[384,1536]{0,1:T(8,128)(2,1)S(1)} %copy.68) | copy-start | bytes 3538948
  424.4 477.5 %copy-start.2 = (f32[384,1536]{1,0:T(8,128)}, f32[384,1536]{1,0:T(8,128)S(1)}, u32[]{:S(2)}) copy-start(f32[384,1536]{1,0:T(8,128)S(1)} %get-tuple-element.49) | copy-start | bytes 7077892
  918.1 279.3 %reduce-scatter.18.cloned.1.call-start = ((), (), s32[]{:S(2)}) async-start(), calls=%async_computation.20 | async-start | bytes 5013504 | tf_op jit(solution)/shard_map/reduce_scatter | solution.py:227
  930.6 410.2 %reduce-scatter.16.cloned.1.call-start = ((), (), s32[]{:S(2)}) async-start(), calls=%async_computation.19 | async-start | bytes 5013504 | tf_op jit(solution)/shard_map/reduce_scatter | solution.py:224
  948.4 535.3 %reduce-scatter.14.cloned.1.call-start = ((), (), s32[]{:S(2)}) async-start(), calls=%async_computation.18 | async-start | bytes 5013504 | tf_op jit(solution)/shard_map/reduce_scatter | solution.py:221
  984.5 642.2 %reduce-scatter.12.cloned.1.call-start = ((), (), s32[]{:S(2)}) async-start(), calls=%async_computation.17 | async-start | bytes 5013504 | tf_op jit(solution)/shard_map/reduce_scatter | solution.py:218
  997.1 836.9 %reduce-scatter.26.cloned.1.call-start = ((), (), s32[]{:S(2)}) async-start(), calls=%async_computation.24 | async-start | bytes 13369344 | tf_op jit(solution)/shard_map/reduce_scatter | solution.py:156
  1008.5 1033.2 %reduce-scatter.24.cloned.1.call-start = ((), (), s32[]{:S(2)}) async-start(), calls=%async_computation.23 | async-start | bytes 13369344 | tf_op jit(solution)/shard_map/reduce_scatter | solution.py:153
  1019.9 1229.5 %reduce-scatter.22.cloned.1.call-start = ((), (), s32[]{:S(2)}) async-start(), calls=%async_computation.22 | async-start | bytes 13369344 | tf_op jit(solution)/shard_map/reduce_scatter | solution.py:150
  1031.4 1345.7 %reduce-scatter.28.cloned.1.call-start = ((), (), s32[]{:S(2)}) async-start(), calls=%async_computation.25 | async-start | bytes 417792
  1037.0 1367.0 %all-reduce.10.cloned.1.call-start = ((), (), s32[]{:S(2)}) async-start(), calls=%async_computation.26 | async-start | bytes 7667712 | tf_op jit(solution)/shard_map/psum | solution.py:239
  (36 other events, 326.8 us)
Sparse Core Ops, SparseCore 0:
  10.9 83.8 all-gather.11
  97.6 78.7 all-gather.13
  179.2 78.3 all-gather.9
  260.2 78.3 all-gather.15
  341.3 78.3 all-gather.17
  422.3 150.0 all-gather.21
  575.2 149.5 all-gather.19
  727.6 149.5 all-gather.23
  918.3 136.5 reduce-scatter.19
  1059.9 137.4 reduce-scatter.17
  1202.6 138.0 reduce-scatter.15
  1345.8 137.8 reduce-scatter.13
  1488.8 137.8 reduce-scatter.11
  1632.2 201.6 reduce-scatter.25
  1839.5 202.1 reduce-scatter.23
  2047.2 202.1 reduce-scatter.21
  2254.5 122.4 reduce-scatter.27
  2379.7 24.2 all-reduce.9
where the time goes:
time: 2430 us; the launch traced here: 2420 us
  waiting for transfers between devices  1940 us (80%)
  matrix products  243 us (10%)
  blocking collectives  166 us (7%)
  other arithmetic  30.7 us (1%)
    reduce_scatter x1, waiting for transfers between devices, local(): lax.psum_scatter(grad_up_w.astype(jnp.bfloat16), 'shard', scatter_dimensi...  208 us
    reduce_scatter x1, waiting for transfers between devices, local(): lax.psum_scatter(grad_gate_w.astype(jnp.bfloat16), 'shard', scatter_dimen...  208 us
    reduce_scatter x1, waiting for transfers between devices, local(): lax.psum_scatter(grad_down.astype(jnp.bfloat16), 'shard', scatter_dimensi...  207 us
    all_gather x1, waiting for transfers between devices, local(): up_part = lax.all_gather(w_up, 'shard', axis=0, tiled=True)  146 us
    reduce_scatter x1, waiting for transfers between devices, local(): lax.psum_scatter(grad_value_w.astype(jnp.bfloat16), 'shard', scatter_dime...  143 us
    reduce_scatter x1, waiting for transfers between devices, local(): lax.psum_scatter(grad_query_w.astype(jnp.bfloat16), 'shard', scatter_dime...  143 us
    reduce_scatter x1, waiting for transfers between devices, local(): lax.psum_scatter(grad_key_w.astype(jnp.bfloat16), 'shard', scatter_dimens...  143 us
    all_gather x1, waiting for transfers between devices, local(): gate_part = lax.all_gather(w_gate, 'shard', axis=0, tiled=True)  142 us
  transfers between devices with their start and end apart: 18, of which 16 were waited for; matrix products, arithmetic and copies ran while one was open for 10% of the time, Pallas kernels for 0%

commit v1 on v0

--- a/solution.py
+++ b/solution.py
@@ -9,6 +9,27 @@
 NC = 4
 EPS = 1e-06
 NEGATIVE = -1e30
+
+
+def collect(shard, axis, dim):
+    size, index, rows = (lax.axis_size(axis), lax.axis_index(axis), shard.shape[dim])
+    right = [(i, (i + 1) % size) for i in range(size)]
+    left = [(i, (i - 1) % size) for i in range(size)]
+    filled = jnp.zeros((*shard.shape[:dim], size * rows, *shard.shape[dim + 1 :]), shard.dtype)
+    filled = lax.dynamic_update_slice_in_dim(filled, shard, index * rows, axis=dim)
+    from_left = from_right = shard
+    middle = size // 2
+    for step in range(1, middle + 1):
+        from_left = lax.ppermute(from_left, axis, right)
+        filled = lax.dynamic_update_slice_in_dim(
+            filled, from_left, (index - step) % size * rows, axis=dim
+        )
+        if step < size - middle:
+            from_right = lax.ppermute(from_right, axis, left)
+            filled = lax.dynamic_update_slice_in_dim(
+                filled, from_right, (index + step) % size * rows, axis=dim
+            )
+    return filled
 
 
 def chain_mask(prompt_ids, offsets):
@@ -115,7 +136,7 @@
     ).reshape(row_count, model_width)
     gate_open = jax.nn.sigmoid(outgate_pre)
     gated_low = (attended * gate_open).astype(jnp.bfloat16)
-    branch_attn = matmul(gated_low, lax.all_gather(w_output, "shard", axis=0, tiled=True))
+    branch_attn = matmul(gated_low, collect(w_output, "shard", 0))
     residual = inputs + branch_attn
     scaled2, inverse2 = normalize(residual)
     gain_part = lax.all_gather(ffn_gain, "shard", axis=0, tiled=True)

time: 2430 us -> 2470 us (1.016)
  starting transfers between devices: 0.97 us -> 41 us
    reduce_scatter x1, waiting for transfers between devices: 0.01 us -> 143 us  [local(): lax.psum_scatter(grad_output_w.astype(jnp.bfloat16), 'shard', scatter_dim...]
    reduce_scatter x1, waiting for transfers between devices: 143 us -> 8.03 us  [local(): lax.psum_scatter(grad_query_w.astype(jnp.bfloat16), 'shard', scatter_dime...]
    all_gather x1, waiting for transfers between devices: 74.1 us -> 0.01 us  [local(): value_part = lax.all_gather(w_value, 'shard', axis=0, tiled=True)]
    ppermute x0 -> x15, waiting for transfers between devices: none -> 65.7 us  [the longest x8 53.1 us: collect(): from_left = lax.ppermute(from_left, axis, right)]
    ppermute x0 -> x15, starting transfers between devices: none -> 40 us  [the longest x7 21.6 us: collect(): from_right = lax.ppermute(from_right, axis, left)]
    reduce_scatter x1, waiting for transfers between devices: 110 us -> 143 us  [local(): lax.psum_scatter(grad_outgate_w.astype(jnp.bfloat16), 'shard', scatter_di...]
    all_gather x1, waiting for transfers between devices: 74.6 us -> 44.3 us  [local(): lax.all_gather(w_output, 'shard', axis=0, tiled=True)]
  transfers between devices with their start and end apart: 18 -> 33, of which waited for: 16 -> 25; matrix products, arithmetic and copies ran while one was open for 10% -> 10% of each run, Pallas kernels for 0% -> 0%
where the time goes in v1:
time: 2470 us
  waiting for transfers between devices  1940 us (79%)
  matrix products  245 us (10%)
  blocking collectives  166 us (7%)
  starting transfers between devices  41 us (2%)
  local copies, waits for them, and re-layouts  33.1 us (1%)
  other arithmetic  29.8 us (1%)
    reduce_scatter x1, waiting for transfers between devices, local(): lax.psum_scatter(grad_up_w.astype(jnp.bfloat16), 'shard', scatter_dimensi...  208 us
    reduce_scatter x1, waiting for transfers between devices, local(): lax.psum_scatter(grad_down.astype(jnp.bfloat16), 'shard', scatter_dimensi...  208 us
    reduce_scatter x1, waiting for transfers between devices, local(): lax.psum_scatter(grad_gate_w.astype(jnp.bfloat16), 'shard', scatter_dimen...  207 us
    reduce_scatter x1, waiting for transfers between devices, local(): lax.psum_scatter(grad_output_w.astype(jnp.bfloat16), 'shard', scatter_dim...  143 us
    reduce_scatter x1, waiting for transfers between devices, local(): lax.psum_scatter(grad_outgate_w.astype(jnp.bfloat16), 'shard', scatter_di...  143 us
    reduce_scatter x1, waiting for transfers between devices, local(): lax.psum_scatter(grad_key_w.astype(jnp.bfloat16), 'shard', scatter_dimens...  143 us
    reduce_scatter x1, waiting for transfers between devices, local(): lax.psum_scatter(grad_value_w.astype(jnp.bfloat16), 'shard', scatter_dime...  143 us
    all_gather x1, waiting for transfers between devices, local(): lax.all_gather(w_down, 'shard', axis=0, tiled=True)  142 us
  transfers between devices with their start and end apart: 33, of which 25 were waited for; matrix products, arithmetic and copies ran while one was open for 10% of the time, Pallas kernels for 0%

profile of v1, /device:TPU:0, one launch (start us, length us, event | category | flops | bytes accessed | tf_op | source)
XLA Modules:
  0.0 2469.0 jit_solution(5328671414272763971)
XLA Ops:
  21.0 44.5 %all-reduce.5 = (bf16[1536]{0:T(1024)(128)(2,1)S(1)}, bf16[1536]{0:T(1024)(128)(2,1)S(1)}) all-reduce(bf16[1536]{0:T(1024)(128)(2,1)S(1)} %dynamic-update-slice, bf16[1536]{0:T(1024)(128)(2,1)S(1)} %dynamic-update-slice.1), channel_id=1, replica_groups=mesh['rep'=2,'shard'=16] {'shard'}, use_global_device_ids=true, to_apply=%add | all-reduce | flops 3072 | bytes 12288
  66.0 37.6 %all-gather = bf16[16,96,24]{1,2,0:T(8,128)(2,1)S(1)} all-gather(bf16[1,96,24]{1,2,0:T(8,128)(2,1)S(1)} %bitcast.93), channel_id=1, replica_groups=mesh['rep'=2,'shard'=16] {'shard'}, dimensions={0}, use_global_device_ids=true | all-gather | bytes 78336 | tf_op jit(solution)/shard_map/all_gather | solution.py:114
  181.3 11.6 collective-permute-done.10
  229.6 70.0 %all-gather.14.cloned.1.call-done = bf16[1536,1536]{1,0:T(8,128)(2,1)} async-done(((bf16[96,1536]{1,0:T(8,128)(2,1)}), bf16[1536,1536]{1,0:T(8,128)(2,1)}) %all-gather.14.cloned.1.call-update) | async-done | bytes 4718608 | tf_op jit(solution)/shard_map/all_gather | solution.py:111
  334.2 46.4 %all-gather.16.cloned.1.call-done = bf16[1536,1536]{1,0:T(8,128)(2,1)} async-done(((bf16[96,1536]{1,0:T(8,128)(2,1)}), bf16[1536,1536]{1,0:T(8,128)(2,1)}) %all-gather.16.cloned.1.call-update) | async-done | bytes 4718608 | tf_op jit(solution)/shard_map/all_gather | solution.py:113
  393.4 139.9 %all-gather.18.cloned.1.call-done = bf16[1536,4096]{1,0:T(8,128)(2,1)} async-done(((bf16[96,4096]{1,0:T(8,128)(2,1)}), bf16[1536,4096]{1,0:T(8,128)(2,1)}) %all-gather.18.cloned.1.call-update) | async-done | bytes 12582928 | tf_op jit(solution)/shard_map/all_gather | solution.py:143
  543.3 142.3 %all-gather.20.cloned.1.call-done = bf16[1536,4096]{1,0:T(8,128)(2,1)} async-done(((bf16[96,4096]{1,0:T(8,128)(2,1)}), bf16[1536,4096]{1,0:T(8,128)(2,1)}) %all-gather.20.cloned.1.call-update) | async-done | bytes 12582928 | tf_op jit(solution)/shard_map/all_gather | solution.py:144
  695.5 142.4 %all-gather.22.cloned.1.call-done = bf16[4096,1536]{1,0:T(8,128)(2,1)} async-done(((bf16[256,1536]{1,0:T(8,128)(2,1)}), bf16[4096,1536]{1,0:T(8,128)(2,1)}) %all-gather.22.cloned.1.call-update) | async-done | bytes 12582928 | tf_op jit(solution)/shard_map/all_gather | solution.py:151
  838.0 15.2 multiply_convert_fusion.1
  874.3 44.3 %all-gather.24.cloned.1.call-done = bf16[1536,1536]{1,0:T(8,128)(2,1)} async-done(((bf16[96,1536]{1,0:T(8,128)(2,1)}), bf16[1536,1536]{1,0:T(8,128)(2,1)}) %all-gather.24.cloned.1.call-update) | async-done | bytes 4718608 | tf_op jit(solution)/shard_map/all_gather | solution.py:185
  928.3 22.3 fusion.83
  1002.2 11.6 convolution_convert_fusion.2
  1013.9 11.3 convolution_convert_fusion.1
  1053.4 40.0 %psum.90 = f32[24]{0:T(128)} all-reduce(f32[24]{0:T(128)S(1)} %get-tuple-element.53), channel_id=1, replica_groups=mesh['rep'=2,'shard'=16] {'rep','shard'}, use_global_device_ids=true, to_apply=%region_25.26 | all-reduce | flops 24 | bytes 192 | tf_op jit(solution)/shard_map/psum | solution.py:209
  1101.4 142.8 %reduce-scatter.14.cloned.1.call-done = bf16[96,1536]{1,0:T(8,128)(2,1)} async-done(((bf16[1536,1536]{1,0:T(8,128)(2,1)}), bf16[96,1536]{1,0:T(8,128)(2,1)}) %reduce-scatter.14.cloned.1.call-update) | async-done | bytes 294928 | tf_op jit(solution)/shard_map/reduce_scatter | solution.py:242
  1244.3 142.6 %reduce-scatter.16.cloned.1.call-done = bf16[96,1536]{1,0:T(8,128)(2,1)} async-done(((bf16[1536,1536]{1,0:T(8,128)(2,1)}), bf16[96,1536]{1,0:T(8,128)(2,1)}) %reduce-scatter.16.cloned.1.call-update) | async-done | bytes 294928 | tf_op jit(solution)/shard_map/reduce_scatter | solution.py:245
  1386.9 142.9 %reduce-scatter.18.cloned.1.call-done = bf16[96,1536]{1,0:T(8,128)(2,1)} async-done(((bf16[1536,1536]{1,0:T(8,128)(2,1)}), bf16[96,1536]{1,0:T(8,128)(2,1)}) %reduce-scatter.18.cloned.1.call-update) | async-done | bytes 294928 | tf_op jit(solution)/shard_map/reduce_scatter | solution.py:248
  1529.8 143.4 %reduce-scatter.20.cloned.1.call-done = bf16[96,1536]{1,0:T(8,128)(2,1)} async-done(((bf16[1536,1536]{1,0:T(8,128)(2,1)}), bf16[96,1536]{1,0:T(8,128)(2,1)}) %reduce-scatter.20.cloned.1.call-update) | async-done | bytes 294928 | tf_op jit(solution)/shard_map/reduce_scatter | solution.py:254
  1673.2 207.2 %reduce-scatter.22.cloned.1.call-done = bf16[96,4096]{1,0:T(8,128)(2,1)} async-done(((bf16[1536,4096]{1,0:T(8,128)(2,1)}), bf16[96,4096]{1,0:T(8,128)(2,1)}) %reduce-scatter.22.cloned.1.call-update) | async-done | bytes 786448 | tf_op jit(solution)/shard_map/reduce_scatter | solution.py:171
  1880.3 207.9 %reduce-scatter.24.cloned.1.call-done = bf16[96,4096]{1,0:T(8,128)(2,1)} async-done(((bf16[1536,4096]{1,0:T(8,128)(2,1)}), bf16[96,4096]{1,0:T(8,128)(2,1)}) %reduce-scatter.24.cloned.1.call-update) | async-done | bytes 786448 | tf_op jit(solution)/shard_map/reduce_scatter | solution.py:174
  2088.2 207.8 %reduce-scatter.26.cloned.1.call-done = bf16[256,1536]{1,0:T(8,128)(2,1)} async-done(((bf16[4096,1536]{1,0:T(8,128)(2,1)}), bf16[256,1536]{1,0:T(8,128)(2,1)}) %reduce-scatter.26.cloned.1.call-update) | async-done | bytes 786448 | tf_op jit(solution)/shard_map/reduce_scatter | solution.py:177
  2309.0 41.8 %all-reduce.4 = (bf16[1536]{0:T(1024)(128)(2,1)}, bf16[1536]{0:T(1024)(128)(2,1)}) all-reduce(bf16[1536]{0:T(1024)(128)(2,1)S(1)} %get-tuple-element.18, bf16[1536]{0:T(1024)(128)(2,1)} %get-tuple-element.16), channel_id=2, replica_groups=mesh['rep'=2,'shard'=16] {'shard'}, use_global_device_ids=true, to_apply=%region_12.13.clone | all-reduce | flops 3072 | bytes 12288
  2366.6 56.9 %reduce-scatter.28.cloned.1.call-done = bf16[96,24]{1,0:T(8,128)(2,1)} async-done(((bf16[1536,24]{1,0:T(8,128)(2,1)}), bf16[96,24]{1,0:T(8,128)(2,1)}) %reduce-scatter.28.cloned.1.call-update) | async-done | bytes 4624
  2428.5 22.1 all-reduce.10.cloned.1.call-done
  (244 shorter events, 357.7 us)
Async XLA Ops:
  7.2 211.4 %all-gather.10.cloned.1.call-start = ((), (), s32[]{:S(2)}) async-start(), calls=%async_computation.9 | async-start | bytes 5013504 | tf_op jit(solution)/shard_map/all_gather | solution.py:112
  8.0 216.4 %all-gather.12.cloned.1.call-start = ((), (), s32[]{:S(2)}) async-start(), calls=%async_computation.10 | async-start | bytes 5013504 | tf_op jit(solution)/shard_map/all_gather | solution.py:110
  8.7 290.8 %all-gather.14.cloned.1.call-start = ((), (), s32[]{:S(2)}) async-start(), calls=%async_computation.11 | async-start | bytes 5013504 | tf_op jit(solution)/shard_map/all_gather | solution.py:111
  9.5 371.1 %all-gather.16.cloned.1.call-start = ((), (), s32[]{:S(2)}) async-start(), calls=%async_computation.12 | async-start | bytes 5013504 | tf_op jit(solution)/shard_map/all_gather | solution.py:113
  10.1 523.2 %all-gather.18.cloned.1.call-start = ((), (), s32[]{:S(2)}) async-start(), calls=%async_computation.13 | async-start | bytes 13369344 | tf_op jit(solution)/shard_map/all_gather | solution.py:143
  10.7 674.9 %all-gather.20.cloned.1.call-start = ((), (), s32[]{:S(2)}) async-start(), calls=%async_computation.14 | async-start | bytes 13369344 | tf_op jit(solution)/shard_map/all_gather | solution.py:144
  11.2 826.7 %all-gather.22.cloned.1.call-start = ((), (), s32[]{:S(2)}) async-start(), calls=%async_computation.15 | async-start | bytes 13369344 | tf_op jit(solution)/shard_map/all_gather | solution.py:151
  12.0 906.7 %all-gather.24.cloned.1.call-start = ((), (), s32[]{:S(2)}) async-start(), calls=%async_computation.16 | async-start | bytes 5013504 | tf_op jit(solution)/shard_map/all_gather | solution.py:185
  12.0 96.9 %collective-permute-start = (bf16[96,1536]{1,0:T(8,128)(2,1)S(1)}, bf16[96,1536]{1,0:T(8,128)(2,1)S(1)}, u32[]{:S(2)}, u32[]{:S(2)}) collective-permute-start(bf16[96,1536]{1,0:T(8,128)(2,1)S(1)} %copy-done.13), channel_id=1, source_target_pairs={{0,1},{1,2},{2,3},{3,4},{4,5},{5,6},{6,7},{7,8},{8,9},{9,10},{10,1... | collective-permute-start | bytes 884744 | tf_op jit(solution)/shard_map/ppermute | solution.py:23
  15.1 95.8 %collective-permute-start.1 = (bf16[96,1536]{1,0:T(8,128)(2,1)S(1)}, bf16[96,1536]{1,0:T(8,128)(2,1)S(1)}, u32[]{:S(2)}, u32[]{:S(2)}) collective-permute-start(bf16[96,1536]{1,0:T(8,128)(2,1)S(1)} %copy-done.13), channel_id=1, source_target_pairs={{0,15},{1,0},{2,1},{3,2},{4,3},{5,4},{6,5},{7,6},{8,7},{9,8},{10,9... | collective-permute-start | bytes 884744 | tf_op jit(solution)/shard_map/ppermute | solution.py:28
  19.1 1082.3 %reduce-scatter.12.cloned.1.call-start = ((), (), s32[]{:S(2)}) async-start(), calls=%async_computation.17 | async-start | bytes 5013504 | tf_op jit(solution)/shard_map/reduce_scatter | solution.py:239
  156.2 18.0 collective-permute-start.8
  158.7 18.0 collective-permute-start.9
  174.2 18.7 collective-permute-start.10
  176.7 25.7 %collective-permute-start.11 = (bf16[96,1536]{1,0:T(8,128)(2,1)S(1)}, bf16[96,1536]{1,0:T(8,128)(2,1)S(1)}, u32[]{:S(2)}, u32[]{:S(2)}) collective-permute-start(bf16[96,1536]{1,0:T(8,128)(2,1)S(1)} %collective-permute-done.9), channel_id=1, source_target_pairs={{0,15},{1,0},{2,1},{3,2},{4,3},{5,4},{6,5},{7,6},{8,7},{9,8},{10,9... | collective-permute-start | bytes 884744 | tf_op jit(solution)/shard_map/ppermute | solution.py:28
  963.2 281.1 %reduce-scatter.14.cloned.1.call-start = ((), (), s32[]{:S(2)}) async-start(), calls=%async_computation.18 | async-start | bytes 5013504 | tf_op jit(solution)/shard_map/reduce_scatter | solution.py:242
  976.9 410.0 %reduce-scatter.16.cloned.1.call-start = ((), (), s32[]{:S(2)}) async-start(), calls=%async_computation.19 | async-start | bytes 5013504 | tf_op jit(solution)/shard_map/reduce_scatter | solution.py:245
  990.6 539.1 %reduce-scatter.18.cloned.1.call-start = ((), (), s32[]{:S(2)}) async-start(), calls=%async_computation.20 | async-start | bytes 5013504 | tf_op jit(solution)/shard_map/reduce_scatter | solution.py:248
  996.5 676.7 %reduce-scatter.20.cloned.1.call-start = ((), (), s32[]{:S(2)}) async-start(), calls=%async_computation.21 | async-start | bytes 5013504 | tf_op jit(solution)/shard_map/reduce_scatter | solution.py:254
  1002.2 878.2 %reduce-scatter.22.cloned.1.call-start = ((), (), s32[]{:S(2)}) async-start(), calls=%async_computation.22 | async-start | bytes 13369344 | tf_op jit(solution)/shard_map/reduce_scatter | solution.py:171
  1013.8 1074.4 %reduce-scatter.24.cloned.1.call-start = ((), (), s32[]{:S(2)}) async-start(), calls=%async_computation.23 | async-start | bytes 13369344 | tf_op jit(solution)/shard_map/reduce_scatter | solution.py:174
  1025.2 1270.8 %reduce-scatter.26.cloned.1.call-start = ((), (), s32[]{:S(2)}) async-start(), calls=%async_computation.24 | async-start | bytes 13369344 | tf_op jit(solution)/shard_map/reduce_scatter | solution.py:177
  1036.6 1386.9 %reduce-scatter.28.cloned.1.call-start = ((), (), s32[]{:S(2)}) async-start(), calls=%async_computation.25 | async-start | bytes 417792
  1042.3 1408.3 %all-reduce.10.cloned.1.call-start = ((), (), s32[]{:S(2)}) async-start(), calls=%async_computation.26 | async-start | bytes 7667712 | tf_op jit(solution)/shard_map/psum | solution.py:260
  (50 other events, 1447.6 us)
Sparse Core Ops, SparseCore 0:
  10.8 89.8 all-gather.9
  103.5 111.4 all-gather.11
  217.9 81.6 all-gather.13
  302.2 78.3 all-gather.15
  383.2 150.0 all-gather.17
  535.9 149.5 all-gather.19
  688.3 149.5 all-gather.21
  840.8 77.8 all-gather.23
  963.3 138.0 reduce-scatter.11
  1106.5 137.7 reduce-scatter.13
  1249.5 137.4 reduce-scatter.15
  1391.9 137.8 reduce-scatter.17
  1535.0 138.1 reduce-scatter.19
  1678.7 201.6 reduce-scatter.21
  1885.8 202.3 reduce-scatter.23
  2093.7 202.2 reduce-scatter.25
  2301.1 122.4 reduce-scatter.27
  2426.3 24.2 all-reduce.9
